TPU v7x, 128 devices: a whole 4x4x4 slice. The times are simulated.
128 devices in a mesh: slab: 64 (over z, y, x), tile: 2 (over core).
Axes of the slice: x: 4, y: 4, z: 4, core: 2. Of those that a mesh axis runs over, the one named last changes fastest.
Arguments:
- samples: float32 [64, 256, 32, 256], P('slab', None, 'tile'), may hold values from -6 to 6
- counts: int32 [64, 256, 32], P('slab', None, 'tile'), may hold values from 1 to 4
- w_in: float32 [64, 64, 256], P('slab'), may hold values from -0.75 to 0.75
- b_in: float32 [64, 256], P('slab'), may hold values from -3 to 3
- w_color: float32 [64, 256, 128], P('slab'), may hold values from -0.375 to 0.375
- b_color: float32 [64, 128], P('slab'), may hold values from -3 to 3
- w_density: float32 [64, 256], P('slab'), may hold values from -0.375 to 0.375
- b_density: float32 [64], P('slab'), may hold values from -1 to 1
- conv_a: bfloat16 [3, 3, 128, 128], replicated, may hold values from -0.1875 to 0.1875
- bias_a: float32 [128], replicated, may hold values from -3 to 3
- conv_b: bfloat16 [3, 3, 128, 128], replicated, may hold values from -0.1875 to 0.1875
- bias_b: float32 [128], replicated, may hold values from -3 to 3
Outputs:
- decoded: bfloat16 [256, 32, 128], P('slab', 'tile')
- front: float32 [64, 256, 32], P('slab', None, 'tile')
All inputs are finite; a program needn't handle non-finite values.
Results may differ from a plain program's by a relative error of at most 0.006.
Values may be sent and summed in bfloat16 or wider, within the bound.
No kernel may reach another device: no remote copies, remote signals or barrier semaphores. Data moves between devices by JAX's collectives and lax.ppermute only.
A program may use at most 128 MiB of HBM per device.

v0:
```python
import jax
import jax.numpy as jnp
from jax import lax
from jax.sharding import PartitionSpec as P

F = 64
K = 4


def padded_2(cells, sides, width):
    for axis, dim in sides:
        count = lax.axis_size(axis)
        ends = count - 1
        head = lax.slice_in_dim(cells, 0, width, axis=dim)
        tail = lax.slice_in_dim(cells, cells.shape[dim] - width, cells.shape[dim], axis=dim)
        cells = jnp.concatenate(
            [
                lax.ppermute(tail, axis, [(i, (i + 1) % count) for i in range(ends)]),
                cells,
                lax.ppermute(head, axis, [((i + 1) % count, i) for i in range(ends)]),
            ],
            axis=dim,
        )
    return cells


def prefix_2(part, axis, combine, identity):
    place = lax.axis_index(axis)
    gathered = lax.all_gather(part, axis)
    state = jnp.zeros_like(part) + jnp.asarray(identity, part.dtype)

    def one(turn, state):
        return combine(state, lax.dynamic_index_in_dim(gathered, turn, 0, False))

    return lax.fori_loop(0, place, one, state)


def hidden_units(inputs, w_in, b_in):
    shaped = inputs.reshape(inputs.shape[:-1] + (K, F))
    return jax.nn.relu(
        jnp.einsum("rwkf,fh->rwkh", shaped, w_in, precision=lax.Precision.HIGHEST) + b_in
    )


def densities(hidden_act, w_density, b_density, live_count):
    before = (
        jnp.einsum("rwkh,h->rwk", hidden_act, w_density, precision=lax.Precision.HIGHEST)
        + b_density
    )
    slots = lax.broadcasted_iota(jnp.int32, before.shape, 2)
    return jnp.where(slots < live_count[..., None], jax.nn.softplus(before), 0.0)


def sample_weights(density, front, total):
    scaled = density / total[..., None]
    earlier = jnp.cumsum(scaled, axis=2) - scaled
    return jnp.exp(-front[..., None] - earlier) * (1.0 - jnp.exp(-scaled))


def partial_image(hidden_act, weight, w_color, b_color):
    color = (
        jnp.einsum("rwkh,hc->rwkc", hidden_act, w_color, precision=lax.Precision.HIGHEST) + b_color
    )
    return jnp.einsum("rwk,rwkc->rwc", weight, color, precision=lax.Precision.HIGHEST)


def add_pair(earlier, later):
    return earlier + later


def convolve(padded, kernel, out_rows, out_cols):
    result = jnp.zeros((out_rows, out_cols, kernel.shape[3]), jnp.float32)
    for row_shift in range(3):
        for col_shift in range(3):
            window = padded[row_shift : row_shift + out_rows, col_shift : col_shift + out_cols]
            result = result + jnp.einsum(
                "rwc,cd->rwd",
                window,
                kernel[row_shift, col_shift],
                preferred_element_type=jnp.float32,
            )
    return result


def strip_edges(field):
    return padded_2(field, (("slab", 0), ("tile", 1)), 1)


def body(
    samples,
    counts,
    w_in,
    b_in,
    w_color,
    b_color,
    w_density,
    b_density,
    conv_a,
    bias_a,
    conv_b,
    bias_b,
):
    slab_count = lax.axis_size("slab")
    height = samples.shape[1]
    tile_cols = samples.shape[2]
    strip_rows = height // slab_count
    hidden_act = hidden_units(samples[0], w_in[0], b_in[0])
    density = densities(hidden_act, w_density[0], b_density[0], counts[0])
    depth = jnp.sum(density, axis=2)
    prefix = prefix_2(depth, "slab", add_pair, jnp.zeros_like(depth))
    total = lax.psum(depth, "slab")
    front = prefix / total
    weight = sample_weights(density, front, total)
    image = lax.psum_scatter(
        partial_image(hidden_act, weight, w_color[0], b_color[0]),
        "slab",
        scatter_dimension=0,
        tiled=True,
    ).astype(jnp.bfloat16)
    first_pad = strip_edges(image)
    hidden_map = jax.nn.relu(convolve(first_pad, conv_a, strip_rows, tile_cols) + bias_a).astype(
        jnp.bfloat16
    )
    second_pad = strip_edges(hidden_map)
    decoded = (convolve(second_pad, conv_b, strip_rows, tile_cols) + bias_b).astype(jnp.bfloat16)
    return (decoded, front[None])


def solution(mesh):
    in_specs = (
        P("slab", None, "tile", None),
        P("slab", None, "tile"),
        P("slab", None, None),
        P("slab", None),
        P("slab", None, None),
        P("slab", None),
        P("slab", None),
        P("slab"),
        P(),
        P(),
        P(),
        P(),
    )
    out_specs = (P("slab", "tile", None), P("slab", None, "tile"))
    return jax.shard_map(body, mesh=mesh, in_specs=in_specs, out_specs=out_specs, check_vma=False)
```

profile of v0, /device:TPU:1, one launch (start us, length us, event | category | flops | bytes accessed | tf_op | source)
XLA Modules:
  0.0 851.4 jit_solution(13505761106247215219)
XLA Ops:
  7.2 0.0 copy-start
  7.2 0.0 copy-start.4
  7.2 0.0 all-gather.3.cloned.1.call-start
  7.2 5.3 copy.24
  12.5 15.6 %fusion.32 = f32[256,16,4,256]{3,0,2,1:T(8,128)S(1)} fusion(f32[256,16,4,64]{0,3,2,1:T(8,128)} %bitcast.147, f32[1,64,256]{2,1,0:T(8,128)S(1)} %copy-done.4), kind=kOutput, calls=%fused_computation.42 | convolution fusion | flops 3221225472 | bytes 21037056 | tf_op jit(solution)/shard_map/rwkf,fh->rwkh/dot_general | solution.py:41
  28.1 5.7 copy-done.1
  33.8 0.0 copy-done.6
  33.8 15.2 %fusion.2 = f32[1,256,16,4]{0,1,3,2:T(8,128)} fusion(f32[256,16,4,256]{3,0,2,1:T(8,128)S(1)} %fusion.32, f32[256]{0:T(256)S(1)} %bitcast.153, f32[1,256]{1,0:T(1,128)S(1)} %copy-done.8), kind=kOutput, calls=%fused_computation.5 | convolution fusion | flops 58720256 | bytes 16844800 | tf_op jit(solution)/shard_map/rwkh,h->rwk/dot_general | solution.py:47
  49.1 5.2 copy.28
  54.9 0.0 copy-done.5
  55.0 0.7 fusion.111
  55.6 0.0 all-gather.3.cloned.1.call-update
  55.6 0.0 reduce-scatter.2.cloned.1.call-start
  55.7 296.8 %psum.7 = f32[256,16]{0,1:T(8,128)S(1)} all-reduce(f32[256,16]{0,1:T(8,128)} %fusion.111), channel_id=1, replica_groups=mesh['slab'=64,'tile'=2] {'slab'}, use_global_device_ids=true, to_apply=%region_3.4 | all-reduce | flops 4096 | bytes 32768 | tf_op jit(solution)/shard_map/psum | solution.py:111
  352.5 0.0 copy-done.7
  352.5 18.1 %broadcast_add_fusion = f32[256,16,4,128]{3,0,2,1:T(8,128)} fusion(f32[128]{0:T(128)S(1)} %bitcast.155, f32[256,16,4,256]{3,0,2,1:T(8,128)} %copy-done.1, f32[256]{0:T(256)S(1)} %bitcast.154, f32[1,256,128]{2,1,0:T(8,128)S(1)} %copy-done), kind=kOutput, calls=%fused_computation.12 | convolution fusion | flops 6452936704 | bytes 25298432 | tf_op jit(solution)/shard_map/rwkh,hc->rwkc/dot_general | solution.py:62
  370.6 1.5 copy.34
  372.1 0.6 divide_bitcast_fusion
  372.7 0.2 fusion.29
  372.9 1.1 copy.30
  374.0 0.0 copy-start.2
  374.0 0.0 copy-start.9
  374.1 0.0 copy-start.3
  374.1 0.0 copy-start.10
  374.1 35.2 %fusion.7 = f32[256,16,1,128]{3,2,1,0:T(1,128)} fusion(f32[256,16,4,1]{2,3,1,0:T(1,128)S(1)} %copy.30, f32[256,16,4,128]{3,0,2,1:T(8,128)} %broadcast_add_fusion), kind=kOutput, calls=%fused_computation.10 | convolution fusion | flops 25165824 | bytes 10551296 | tf_op jit(solution)/shard_map/rwk,rwkc->rwc/dot_general | solution.py:64
  409.3 0.0 reduce-scatter.2.cloned.1.call-update
  409.3 356.2 %reduce-scatter.2.cloned.1.call-done = f32[4,16,128]{2,1,0:T(8,128)} async-done(((f32[256,16,128]{2,1,0:T(8,128)}), f32[4,16,128]{2,1,0:T(8,128)}) %reduce-scatter.2.cloned.1.call-update) | async-done | bytes 32784 | tf_op jit(solution)/shard_map/reduce_scatter | solution.py:114
  765.5 0.8 convert_element_type.9
  766.3 1.3 collective-permute-start
  767.6 1.3 collective-permute-start.1
  768.9 0.1 fusion.58
  769.0 0.0 collective-permute-done
  769.0 3.3 collective-permute-done.1
  772.4 1.3 collective-permute-start.2
  773.7 56.3 %collective-permute-start.3 = (bf16[6,1,128]{2,1,0:T(2,128)(2,1)S(1)}, bf16[6,1,128]{2,1,0:T(2,128)(2,1)S(1)}, u32[]{:S(2)}, u32[]{:S(2)}) collective-permute-start(bf16[6,1,128]{2,1,0:T(2,128)(2,1)S(1)} %get-tuple-element.55), channel_id=1, source_target_pairs={{1,0},{3,2},{5,4},{7,6},{9,8},{11,10},{13,12},{15,14},{17,16},{19,... | collective-permute-start | bytes 4616 | tf_op jit(solution)/shard_map/ppermute | solution.py:20
  829.9 0.1 fusion.64
  830.1 0.1 fusion.53
  830.2 0.0 collective-permute-done.2
  830.2 0.5 collective-permute-done.3
  830.8 0.1 fusion.62
  830.9 0.1 fusion.51
  831.0 0.1 fusion.60
  831.1 0.1 fusion.55
  831.3 0.1 fusion.26
  831.4 0.1 fusion.27
  831.6 1.4 collective-permute-start.4
  833.0 1.3 collective-permute-start.5
  834.3 0.0 copy-done.3
  834.3 0.1 fusion.42
  834.4 0.0 collective-permute-done.4
  834.4 2.9 collective-permute-done.5
  837.3 1.3 collective-permute-start.6
  838.6 3.7 collective-permute-start.7
  842.3 0.1 fusion.48
  842.4 0.1 fusion.37
  842.6 0.0 collective-permute-done.6
  842.6 0.5 collective-permute-done.7
  843.1 0.1 fusion.46
  843.3 0.1 fusion.35
  843.4 0.1 fusion.44
  843.5 0.1 fusion.39
  843.7 0.1 fusion.18
  843.8 0.0 copy-done.10
  843.8 0.8 fusion.28
  (19 shorter events, 0.1 us)
Async XLA Ops:
  7.2 345.3 %copy-start = (f32[1,256,128]{2,1,0:T(8,128)S(1)}, f32[1,256,128]{2,1,0:T(8,128)}, u32[]{:S(2)}) copy-start(f32[1,256,128]{2,1,0:T(8,128)} %param.18) | copy-start | bytes 393220
  7.2 5.3 copy-start.4
  7.2 363.4 %all-gather.3.cloned.1.call-start = ((), (), s32[]{:S(2)}) async-start(), calls=%async_computation.2 | async-start | bytes 1064960 | tf_op jit(solution)/shard_map/all_gather | solution.py:29
  12.5 21.3 %copy-start.6 = (f32[1,256]{1,0:T(1,128)S(1)}, f32[1,256]{1,0:T(1,128)}, u32[]{:S(2)}) copy-start(f32[1,256]{1,0:T(1,128)} %param.17) | copy-start | bytes 3076
  12.5 21.3 %copy-start.8 = (f32[1,256]{1,0:T(1,128)S(1)}, f32[1,256]{1,0:T(1,128)}, u32[]{:S(2)}) copy-start(f32[1,256]{1,0:T(1,128)} %param.20) | copy-start | bytes 3076
  28.1 5.7 copy-start.1
  49.1 5.9 copy-start.5
  49.1 303.4 %copy-start.7 = (f32[1,128]{1,0:T(1,128)S(1)}, f32[1,128]{1,0:T(1,128)}, u32[]{:S(2)}) copy-start(f32[1,128]{1,0:T(1,128)} %param.19) | copy-start | bytes 1540
  55.6 709.9 %reduce-scatter.2.cloned.1.call-start = ((), (), s32[]{:S(2)}) async-start(), calls=%async_computation.1 | async-start | bytes 2129920 | tf_op jit(solution)/shard_map/reduce_scatter | solution.py:114
  374.0 394.9 %copy-start.2 = (bf16[3,3,128,128]{3,2,1,0:T(8,128)(2,1)S(1)}, bf16[3,3,128,128]{3,2,1,0:T(8,128)(2,1)}, u32[]{:S(2)}) copy-start(bf16[3,3,128,128]{3,2,1,0:T(8,128)(2,1)} %param.22) | copy-start | bytes 884740
  374.0 457.4 %copy-start.9 = (f32[128]{0:T(128)S(1)}, f32[128]{0:T(128)}, u32[]{:S(2)}) copy-start(f32[128]{0:T(128)} %param.23) | copy-start | bytes 1540
  374.1 460.2 %copy-start.3 = (bf16[3,3,128,128]{3,2,1,0:T(8,128)(2,1)S(1)}, bf16[3,3,128,128]{3,2,1,0:T(8,128)(2,1)}, u32[]{:S(2)}) copy-start(bf16[3,3,128,128]{3,2,1,0:T(8,128)(2,1)} %param.24) | copy-start | bytes 884740
  374.1 469.7 %copy-start.10 = (f32[128]{0:T(128)S(1)}, f32[128]{0:T(128)}, u32[]{:S(2)}) copy-start(f32[128]{0:T(128)} %param.25) | copy-start | bytes 1540
  766.3 2.7 collective-permute-start
  767.6 4.8 collective-permute-start.1
  772.4 57.8 %collective-permute-start.2 = (bf16[6,1,128]{2,1,0:T(2,128)(2,1)S(1)}, bf16[6,1,128]{2,1,0:T(2,128)(2,1)S(1)}, u32[]{:S(2)}, u32[]{:S(2)}) collective-permute-start(bf16[6,1,128]{2,1,0:T(2,128)(2,1)S(1)} %get-tuple-element.54), channel_id=1, source_target_pairs={{0,1},{2,3},{4,5},{6,7},{8,9},{10,11},{12,13},{14,15},{16,17},{18,... | collective-permute-start | bytes 4616 | tf_op jit(solution)/shard_map/ppermute | solution.py:18
  773.7 57.1 %collective-permute-start.3 = (bf16[6,1,128]{2,1,0:T(2,128)(2,1)S(1)}, bf16[6,1,128]{2,1,0:T(2,128)(2,1)S(1)}, u32[]{:S(2)}, u32[]{:S(2)}) collective-permute-start(bf16[6,1,128]{2,1,0:T(2,128)(2,1)S(1)} %get-tuple-element.55), channel_id=1, source_target_pairs={{1,0},{3,2},{5,4},{7,6},{9,8},{11,10},{13,12},{15,14},{17,16},{19,... | collective-permute-start | bytes 4616 | tf_op jit(solution)/shard_map/ppermute | solution.py:20
  831.6 2.8 collective-permute-start.4
  833.0 4.4 collective-permute-start.5
  837.3 5.2 collective-permute-start.6
  838.6 4.5 collective-permute-start.7
Sparse Core Ops, SparseCore 0:
  55.8 64.9 all-gather.2
  409.4 356.0 reduce-scatter.1
where the time goes:
time: 852 us; the launch traced here: 851 us
  waiting for transfers between devices  364 us (43%)
  blocking collectives  297 us (35%)
  matrix products  87.1 us (10%)
  starting transfers between devices  67.8 us (8%)
  local copies, waits for them, and re-layouts  18.9 us (2%)
  between operations  14.9 us (2%)
    reduce_scatter x1, waiting for transfers between devices, body(): lax.psum_scatter(partial_image(hidden_act, weight, w_color[0], b_color[0]...  356 us
    psum x1, blocking collectives, body(): total = lax.psum(depth, 'slab')  297 us
    ppermute x4, starting transfers between devices, padded_2(): lax.ppermute(head, axis, [((i + 1) % count, i) for i in range(ends)])  62.5 us
    dot_general x1, matrix products, partial_image(): jnp.einsum('rwk,rwkc->rwc', weight, color, precision=lax.Precision.HIGHEST)  35.2 us
    dot_general x1, matrix products, partial_image(): jnp.einsum('rwkh,hc->rwkc', hidden_act, w_color, precision=lax.Precision....  18.1 us
  transfers between devices with their start and end apart: 10, of which 5 were waited for; matrix products, arithmetic and copies ran while one was open for 2% of the time, Pallas kernels for 0%

commit v1 on v0

--- a/solution.py
+++ b/solution.py
@@ -108,7 +108,8 @@
     density = densities(hidden_act, w_density[0], b_density[0], counts[0])
     depth = jnp.sum(density, axis=2)
     prefix = prefix_2(depth, "slab", add_pair, jnp.zeros_like(depth))
-    total = lax.psum(depth, "slab")
+    parts = lax.all_gather(depth, "slab")
+    total = jnp.sum(parts, axis=0)
     front = prefix / total
     weight = sample_weights(density, front, total)
     image = lax.psum_scatter(

time: 852 us -> 553 us (0.65)
  blocking collectives: 297 us -> 0 us
    psum x1 -> x0, blocking collectives: 297 us -> none  [body(): total = lax.psum(depth, 'slab')]
    reduce_scatter x1, waiting for transfers between devices: 356 us -> 308 us  [body(): lax.psum_scatter(partial_image(hidden_act, weight, w_color[0], b_color[0]...]
    all_gather x1, waiting for transfers between devices: 0.01 us -> 46.7 us  [prefix_2(): gathered = lax.all_gather(part, axis)]
  transfers between devices with their start and end apart: 10 -> 10, of which waited for: 5 -> 6; matrix products, arithmetic and copies ran while one was open for 2% -> 3% of each run, Pallas kernels for 0% -> 0%
where the time goes in v1:
time: 553 us
  waiting for transfers between devices  362 us (65%)
  matrix products  87.1 us (16%)
  starting transfers between devices  67.1 us (12%)
  local copies, waits for them, and re-layouts  18.9 us (3%)
  between operations  15 us (3%)
    reduce_scatter x1, waiting for transfers between devices, body(): lax.psum_scatter(partial_image(hidden_act, weight, w_color[0], b_color[0]...  308 us
    ppermute x4, starting transfers between devices, padded_2(): lax.ppermute(head, axis, [((i + 1) % count, i) for i in range(ends)])  61.6 us
    all_gather x1, waiting for transfers between devices, prefix_2(): gathered = lax.all_gather(part, axis)  46.7 us
    dot_general x1, matrix products, partial_image(): jnp.einsum('rwk,rwkc->rwc', weight, color, precision=lax.Precision.HIGHEST)  35.2 us
    dot_general x1, matrix products, partial_image(): jnp.einsum('rwkh,hc->rwkc', hidden_act, w_color, precision=lax.Precision....  18.1 us
    dot_general x1, matrix products, hidden_units(): jnp.einsum('rwkf,fh->rwkh', shaped, w_in, precision=lax.Precision.HIGHEST)  15.6 us
    dot_general x1, matrix products, densities(): jnp.einsum('rwkh,h->rwk', hidden_act, w_density, precision=lax.Precision....  15.2 us
    unnamed x24, local copies, waits for them, and re-layouts  12.6 us
  transfers between devices with their start and end apart: 10, of which 6 were waited for; matrix products, arithmetic and copies ran while one was open for 3% of the time, Pallas kernels for 0%

profile of v1, /device:TPU:1, one launch (start us, length us, event | category | flops | bytes accessed | tf_op | source)
XLA Modules:
  0.0 552.7 jit_solution(9292170776986317852)
XLA Ops:
  7.2 0.0 copy-start
  7.2 0.0 copy-start.4
  7.2 0.0 all-gather.3.cloned.1.call-start
  7.2 5.3 copy.23
  12.5 0.0 copy-done.4
  12.5 15.6 %fusion.32 = f32[256,16,4,256]{3,0,2,1:T(8,128)S(1)} fusion(f32[256,16,4,64]{0,3,2,1:T(8,128)} %bitcast.148, f32[1,64,256]{2,1,0:T(8,128)S(1)} %copy-done.4), kind=kOutput, calls=%fused_computation.42 | convolution fusion | flops 3221225472 | bytes 21037056 | tf_op jit(solution)/shard_map/rwkf,fh->rwkh/dot_general | solution.py:41
  28.1 5.7 %copy-done.1 = f32[256,16,4,256]{3,0,2,1:T(8,128)} copy-done((f32[256,16,4,256]{3,0,2,1:T(8,128)}, f32[256,16,4,256]{3,0,2,1:T(8,128)S(1)}, u32[]{:S(2)}) %copy-start.1) | copy-done | bytes 16777240
  33.8 0.0 copy-done.6
  33.8 15.2 %fusion.2 = f32[1,256,16,4]{0,1,3,2:T(8,128)} fusion(f32[256,16,4,256]{3,0,2,1:T(8,128)S(1)} %fusion.32, f32[256]{0:T(256)S(1)} %bitcast.154, f32[1,256]{1,0:T(1,128)S(1)} %copy-done.8), kind=kOutput, calls=%fused_computation.5 | convolution fusion | flops 58720256 | bytes 16844800 | tf_op jit(solution)/shard_map/rwkh,h->rwk/dot_general | solution.py:47
  49.1 5.2 copy.27
  54.9 0.0 copy-done.5
  55.0 0.7 fusion.111
  55.6 0.0 all-gather.3.cloned.1.call-update
  55.6 0.2 reduce-scatter.2.cloned.1.call-start
  55.9 18.1 %broadcast_add_fusion = f32[256,16,4,128]{3,0,2,1:T(8,128)} fusion(f32[128]{0:T(128)S(1)} %bitcast.156, f32[256,16,4,256]{3,0,2,1:T(8,128)} %copy-done.1, f32[256]{0:T(256)S(1)} %bitcast.155, f32[1,256,128]{2,1,0:T(8,128)S(1)} %copy-done), kind=kOutput, calls=%fused_computation.12 | convolution fusion | flops 6452936704 | bytes 25298432 | tf_op jit(solution)/shard_map/rwkh,hc->rwkc/dot_general | solution.py:62
  74.0 46.7 %all-gather.3.cloned.1.call-done = f32[16384,16]{0,1:T(8,128)} async-done(((f32[256,16]{0,1:T(8,128)}), f32[16384,16]{0,1:T(8,128)}) %all-gather.3.cloned.1.call-update) | async-done | bytes 1048592 | tf_op jit(solution)/shard_map/all_gather | solution.py:29
  120.7 1.5 copy.33
  122.3 0.1 bitcast_reduce_fusion
  122.4 0.6 divide_bitcast_fusion
  123.0 0.2 fusion.29
  123.2 1.1 copy.29
  124.3 0.0 copy-start.2
  124.3 0.0 copy-start.9
  124.3 0.0 copy-start.3
  124.3 0.0 copy-start.10
  124.3 35.2 %fusion.7 = f32[256,16,1,128]{3,2,1,0:T(1,128)} fusion(f32[256,16,4,1]{2,3,1,0:T(1,128)S(1)} %copy.29, f32[256,16,4,128]{3,0,2,1:T(8,128)} %broadcast_add_fusion), kind=kOutput, calls=%fused_computation.10 | convolution fusion | flops 25165824 | bytes 10551296 | tf_op jit(solution)/shard_map/rwk,rwkc->rwc/dot_general | solution.py:64
  159.5 0.0 reduce-scatter.2.cloned.1.call-update
  159.6 308.1 %reduce-scatter.2.cloned.1.call-done = f32[4,16,128]{2,1,0:T(8,128)} async-done(((f32[256,16,128]{2,1,0:T(8,128)}), f32[4,16,128]{2,1,0:T(8,128)}) %reduce-scatter.2.cloned.1.call-update) | async-done | bytes 32784 | tf_op jit(solution)/shard_map/reduce_scatter | solution.py:115
  467.7 0.8 convert_element_type.9
  468.4 1.3 collective-permute-start
  469.7 1.3 collective-permute-start.1
  471.0 0.1 fusion.58
  471.2 0.0 collective-permute-done
  471.2 3.3 collective-permute-done.1
  474.5 1.3 collective-permute-start.2
  475.8 55.4 %collective-permute-start.3 = (bf16[6,1,128]{2,1,0:T(2,128)(2,1)S(1)}, bf16[6,1,128]{2,1,0:T(2,128)(2,1)S(1)}, u32[]{:S(2)}, u32[]{:S(2)}) collective-permute-start(bf16[6,1,128]{2,1,0:T(2,128)(2,1)S(1)} %get-tuple-element.51), channel_id=1, source_target_pairs={{1,0},{3,2},{5,4},{7,6},{9,8},{11,10},{13,12},{15,14},{17,16},{19,... | collective-permute-start | bytes 4616 | tf_op jit(solution)/shard_map/ppermute | solution.py:20
  531.2 0.1 fusion.64
  531.3 0.1 fusion.53
  531.4 0.0 collective-permute-done.2
  531.4 0.5 collective-permute-done.3
  532.0 0.1 fusion.62
  532.1 0.1 fusion.51
  532.3 0.1 fusion.60
  532.4 0.1 fusion.55
  532.5 0.1 fusion.26
  532.7 0.0 copy-done.9
  532.7 0.1 fusion.27
  532.9 1.4 collective-permute-start.4
  534.2 1.3 collective-permute-start.5
  535.5 0.1 fusion.42
  535.7 0.0 collective-permute-done.4
  535.7 2.9 collective-permute-done.5
  538.6 1.3 collective-permute-start.6
  539.9 3.7 collective-permute-start.7
  543.6 0.1 fusion.48
  543.7 0.1 fusion.37
  543.8 0.0 collective-permute-done.6
  543.8 0.5 collective-permute-done.7
  544.4 0.1 fusion.46
  544.5 0.1 fusion.35
  544.7 0.1 fusion.44
  544.8 0.1 fusion.39
  544.9 0.1 fusion.18
  545.1 0.8 fusion.28
  (19 shorter events, 0.1 us)
Async XLA Ops:
  7.2 48.7 %copy-start = (f32[1,256,128]{2,1,0:T(8,128)S(1)}, f32[1,256,128]{2,1,0:T(8,128)}, u32[]{:S(2)}) copy-start(f32[1,256,128]{2,1,0:T(8,128)} %param.18) | copy-start | bytes 393220
  7.2 5.3 copy-start.4
  7.2 113.6 %all-gather.3.cloned.1.call-start = ((), (), s32[]{:S(2)}) async-start(), calls=%async_computation.2 | async-start | bytes 1064960 | tf_op jit(solution)/shard_map/all_gather | solution.py:29
  12.5 21.3 %copy-start.6 = (f32[1,256]{1,0:T(1,128)S(1)}, f32[1,256]{1,0:T(1,128)}, u32[]{:S(2)}) copy-start(f32[1,256]{1,0:T(1,128)} %param.17) | copy-start | bytes 3076
  12.5 21.3 %copy-start.8 = (f32[1,256]{1,0:T(1,128)S(1)}, f32[1,256]{1,0:T(1,128)}, u32[]{:S(2)}) copy-start(f32[1,256]{1,0:T(1,128)} %param.20) | copy-start | bytes 3076
  28.1 5.7 %copy-start.1 = (f32[256,16,4,256]{3,0,2,1:T(8,128)}, f32[256,16,4,256]{3,0,2,1:T(8,128)S(1)}, u32[]{:S(2)}) copy-start(f32[256,16,4,256]{3,0,2,1:T(8,128)S(1)} %fusion.32) | copy-start | bytes 50331652
  49.1 5.9 %copy-start.5 = (s32[1,256,16]{1,2,0:T(8,128)S(1)}, s32[1,256,16]{1,2,0:T(8,128)}, u32[]{:S(2)}) copy-start(s32[1,256,16]{1,2,0:T(8,128)} %param.15) | copy-start | bytes 49156
  49.1 6.8 %copy-start.7 = (f32[1,128]{1,0:T(1,128)S(1)}, f32[1,128]{1,0:T(1,128)}, u32[]{:S(2)}) copy-start(f32[1,128]{1,0:T(1,128)} %param.19) | copy-start | bytes 1540
  55.6 412.0 %reduce-scatter.2.cloned.1.call-start = ((), (), s32[]{:S(2)}) async-start(), calls=%async_computation.1 | async-start | bytes 2129920 | tf_op jit(solution)/shard_map/reduce_scatter | solution.py:115
  124.3 346.7 %copy-start.2 = (bf16[3,3,128,128]{3,2,1,0:T(8,128)(2,1)S(1)}, bf16[3,3,128,128]{3,2,1,0:T(8,128)(2,1)}, u32[]{:S(2)}) copy-start(bf16[3,3,128,128]{3,2,1,0:T(8,128)(2,1)} %param.22) | copy-start | bytes 884740
  124.3 408.4 %copy-start.9 = (f32[128]{0:T(128)S(1)}, f32[128]{0:T(128)}, u32[]{:S(2)}) copy-start(f32[128]{0:T(128)} %param.23) | copy-start | bytes 1540
  124.3 411.2 %copy-start.3 = (bf16[3,3,128,128]{3,2,1,0:T(8,128)(2,1)S(1)}, bf16[3,3,128,128]{3,2,1,0:T(8,128)(2,1)}, u32[]{:S(2)}) copy-start(bf16[3,3,128,128]{3,2,1,0:T(8,128)(2,1)} %param.24) | copy-start | bytes 884740
  124.3 420.7 %copy-start.10 = (f32[128]{0:T(128)S(1)}, f32[128]{0:T(128)}, u32[]{:S(2)}) copy-start(f32[128]{0:T(128)} %param.25) | copy-start | bytes 1540
  468.4 2.7 collective-permute-start
  469.7 4.8 collective-permute-start.1
  474.5 57.0 %collective-permute-start.2 = (bf16[6,1,128]{2,1,0:T(2,128)(2,1)S(1)}, bf16[6,1,128]{2,1,0:T(2,128)(2,1)S(1)}, u32[]{:S(2)}, u32[]{:S(2)}) collective-permute-start(bf16[6,1,128]{2,1,0:T(2,128)(2,1)S(1)} %get-tuple-element.50), channel_id=1, source_target_pairs={{0,1},{2,3},{4,5},{6,7},{8,9},{10,11},{12,13},{14,15},{16,17},{18,... | collective-permute-start | bytes 4616 | tf_op jit(solution)/shard_map/ppermute | solution.py:18
  475.8 56.2 %collective-permute-start.3 = (bf16[6,1,128]{2,1,0:T(2,128)(2,1)S(1)}, bf16[6,1,128]{2,1,0:T(2,128)(2,1)S(1)}, u32[]{:S(2)}, u32[]{:S(2)}) collective-permute-start(bf16[6,1,128]{2,1,0:T(2,128)(2,1)S(1)} %get-tuple-element.51), channel_id=1, source_target_pairs={{1,0},{3,2},{5,4},{7,6},{9,8},{11,10},{13,12},{15,14},{17,16},{19,... | collective-permute-start | bytes 4616 | tf_op jit(solution)/shard_map/ppermute | solution.py:20
  532.9 2.8 collective-permute-start.4
  534.2 4.4 collective-permute-start.5
  538.6 5.2 collective-permute-start.6
  539.9 4.5 collective-permute-start.7
Sparse Core Ops, SparseCore 0:
  55.8 64.9 all-gather.2
  159.7 307.9 reduce-scatter.1
